TPU v7x, 512 devices: a whole 4x8x8 slice. The times are simulated.
512 devices in a mesh: pair: 32 (over y, x), row: 16 (over z, core).
Axes of the slice: x: 4, y: 8, z: 8, core: 2. Of those that a mesh axis runs over, the one named last changes fastest.
Arguments:
- r_factor: float32 [16384, 16384], P(('row', 'pair')), may hold values from -40 to 40, as said below
- block_slots: int32 [256], replicated, may hold values from 0 to 255, as said below
Outputs:
- rotated: float32 [16384, 16384], P('row', 'pair')
- off_ratio: float32 [], replicated
Inputs may be any that keep to these rules, and one draw needn't show every extreme that they name: `block_slots`: each of the 256 column blocks appears exactly once. `r_factor`: entries below the diagonal are zero and the diagonal is positive.
All inputs are finite; a program needn't handle non-finite values.
Results may differ from a plain program's by a relative error of at most 0.0001.
Values sent between devices are 32-bit elements; how exact they have to be, the bound alone decides.
A program may use at most 64 MiB of HBM per device.

v0:
```python
import jax
import jax.numpy as jnp
from jax import lax
from jax.sharding import PartitionSpec as P

BLOCK = 64
ITERS = 3


def passed_along(value, axis, by):
    count = lax.axis_size(axis)
    pairs = [(i, i + by) for i in range(count) if 0 <= i + by < count]
    return lax.ppermute(value, axis, pairs)


def cayley(pair_gram):
    size_n = pair_gram.shape[0]
    diag_vals = jnp.diagonal(pair_gram)
    spread = diag_vals[:, None] - diag_vals[None, :]
    denom = 2.0 * (diag_vals[:, None] ** 2 + diag_vals[None, :] ** 2)
    skew_part = pair_gram * spread / denom
    unit_matrix = jnp.eye(size_n, dtype=pair_gram.dtype)
    minus_part = unit_matrix - skew_part
    system = unit_matrix - jnp.dot(skew_part, skew_part, precision=lax.Precision.HIGHEST)
    product = jnp.dot(minus_part, minus_part, precision=lax.Precision.HIGHEST)
    factor = jnp.linalg.cholesky(system)
    return jax.scipy.linalg.cho_solve((factor, True), product.T).T


def square_sums(rows_part):
    row_ids = jnp.arange(rows_part.shape[1], dtype=jnp.int32)[:, None]
    col_ids = jnp.arange(rows_part.shape[2], dtype=jnp.int32)[None, :]
    on_diag = (row_ids == col_ids)[None, :, :]
    squares = rows_part * rows_part
    return (jnp.sum(jnp.where(on_diag, 0.0, squares)), jnp.sum(jnp.where(on_diag, squares, 0.0)))


def on_device(r_factor, block_slots):
    rows_in, total_cols = r_factor.shape
    blocks = total_cols // BLOCK
    pair_width = 2 * BLOCK
    arranged = jnp.take(r_factor.reshape(rows_in, blocks, BLOCK), block_slots, axis=1)
    arranged = arranged.reshape(rows_in, blocks // 2, pair_width)
    received = lax.all_to_all(arranged, "pair", split_axis=1, concat_axis=0, tiled=True)
    column = jnp.transpose(received, (1, 0, 2))
    local_pairs = column.shape[0]
    rows_here = column.shape[1]
    totals = None
    for sweep in range(ITERS):
        partial_value = jnp.einsum("pri,prj->pij", column, column, precision=lax.Precision.HIGHEST)
        pair_gram = lax.psum(partial_value, "row")
        if sweep == 0:
            off_part, diag_part = square_sums(pair_gram)
            totals = lax.psum((off_part, diag_part), "pair")
        rotation = jax.vmap(cayley)(pair_gram)
        column = jnp.einsum("pri,pij->prj", column, rotation, precision=lax.Precision.HIGHEST)
    upper_half = column[:, :, :BLOCK]
    lower_half = column[:, :, BLOCK:]
    pair_index = lax.axis_index("pair")
    pair_count = lax.axis_size("pair")
    global_ids = pair_index * local_pairs + jnp.arange(local_pairs, dtype=jnp.int32)
    last_id = pair_count * local_pairs - 1
    first_mask = (global_ids == 0)[:, None, None]
    last_mask = (global_ids == last_id)[:, None, None]
    forward = jnp.where(first_mask, lower_half, upper_half)
    came_up = passed_along(forward[local_pairs - 1], "pair", 1)
    came_down = passed_along(lower_half[0], "pair", -1)
    before = jnp.concatenate([came_up[None], forward[: local_pairs - 1]], axis=0)
    after = jnp.concatenate([lower_half[1:], came_down[None]], axis=0)
    new_upper = jnp.where(first_mask, upper_half, before)
    new_lower = jnp.where(last_mask, upper_half, after)
    joined = jnp.concatenate([new_upper, new_lower], axis=2)
    rotated = jnp.transpose(joined, (1, 0, 2)).reshape(rows_here, local_pairs * pair_width)
    off_ratio = jnp.sqrt(totals[0] / totals[1])
    return (rotated, off_ratio)


def solution(mesh):
    in_specs = (P(("row", "pair"), None), P())
    out_specs = (P("row", "pair"), P())
    return jax.shard_map(
        on_device, mesh=mesh, in_specs=in_specs, out_specs=out_specs, check_vma=False
    )
```

profile of v0, /device:TPU:32, one launch (start us, length us, event | category | flops | bytes accessed | tf_op | source)
XLA Modules:
  0.0 870.0 jit_solution(1644041194459896223)
XLA Ops:
  7.2 0.7 compare_and_fusion
  7.9 0.7 compare_select_fusion
  8.5 0.2 broadcast_in_dim.98
  8.9 4.3 reshape.87
  13.2 6.5 copy.172
  19.7 5.0 gather_fusion
  24.7 6.5 copy.173
  31.3 3.3 gather.17
  34.5 0.2 broadcast_select_fusion
  34.7 2.5 copy.174
  37.3 9.8 %all-to-all-start = ((f32[32,128,128]{2,0,1:T(8,128)}), f32[32,128,128]{2,0,1:T(8,128)S(1)}, u32[]{:S(2)}, u32[]{:S(2)}) async-start(f32[32,128,128]{2,0,1:T(8,128)} %copy.174), calls=%async_computation | async-start | bytes 4194304 | tf_op jit(solution)/shard_map/all_to_all | solution.py:44
  47.1 0.3 all-reduce.5.cloned.1.call-start
  47.4 46.9 %all-to-all-done = f32[32,128,128]{2,0,1:T(8,128)S(1)} async-done(((f32[32,128,128]{2,0,1:T(8,128)}), f32[32,128,128]{2,0,1:T(8,128)S(1)}, u32[]{:S(2)}, u32[]{:S(2)}) %all-to-all-start) | async-done | bytes 2097184 | tf_op jit(solution)/shard_map/all_to_all | solution.py:44
  94.3 1.3 copy-done.3
  95.6 1.8 copy.175
  97.4 4.3 fusion.33
  101.8 119.5 %all-reduce.5.cloned.1.call-done = f32[4,128,128]{1,2,0:T(8,128)} async-done(((f32[4,128,128]{1,2,0:T(8,128)}), f32[4,128,128]{1,2,0:T(8,128)}) %all-reduce.5.cloned.1.call-update) | async-done | bytes 262160 | tf_op jit(solution)/shard_map/psum | solution.py:51
  221.3 8.5 copy.178
  229.7 1.8 gather_fusion.1
  231.6 0.7 convolution_subtract_fusion.2
  232.3 0.1 copy.183
  232.4 46.9 %custom-call.18 = f32[4,128,128]{2,1,0:T(8,128)S(1)} custom-call(f32[4,128,128]{2,1,0:T(8,128)S(1)} %fusion.14), custom_call_target="Cholesky" | custom-call | tf_op jit(solution)/shard_map/vmap(jit(cholesky))/cholesky | solution.py:26
  279.6 39.7 %custom-call.19 = f32[4,1,128,128]{2,3,1,0:T(8,128)S(1)} custom-call(f32[4,1,128,128]{3,2,1,0:T(8,128)S(1)} %select_bitcast_fusion.2), custom_call_target="InvertDiagBlocksLowerTriangular" | custom-call | tf_op jit(solution)/shard_map/vmap(jit(_cho_solve))/triangular_solve | solution.py:27
  319.3 0.6 fusion.19
  320.0 0.6 fusion.12
  320.6 0.4 fusion.10
  321.0 1.9 fusion.34
  323.0 1.3 copy-done
  324.3 4.3 fusion.35
  328.6 116.2 %all-reduce.7.cloned.1.call-done = f32[4,128,128]{1,2,0:T(8,128)} async-done(((f32[4,128,128]{1,2,0:T(8,128)}), f32[4,128,128]{1,2,0:T(8,128)}) %all-reduce.7.cloned.1.call-update) | async-done | bytes 262160 | tf_op jit(solution)/shard_map/psum | solution.py:51
  444.8 8.5 copy.188
  453.3 1.8 gather_fusion.2
  455.2 0.7 convolution_subtract_fusion.1
  455.9 0.1 copy.193
  456.0 46.9 %custom-call.20 = f32[4,128,128]{2,1,0:T(8,128)S(1)} custom-call(f32[4,128,128]{2,1,0:T(8,128)S(1)} %fusion.9), custom_call_target="Cholesky" | custom-call | tf_op jit(solution)/shard_map/vmap(jit(cholesky))/cholesky | solution.py:26
  503.2 39.5 %custom-call.21 = f32[4,1,128,128]{2,3,1,0:T(8,128)S(1)} custom-call(f32[4,1,128,128]{3,2,1,0:T(8,128)S(1)} %select_bitcast_fusion.1), custom_call_target="InvertDiagBlocksLowerTriangular" | custom-call | tf_op jit(solution)/shard_map/vmap(jit(_cho_solve))/triangular_solve | solution.py:27
  542.7 0.6 fusion.17
  543.4 0.6 fusion.7
  544.0 0.4 fusion.5
  544.4 3.5 fusion.36
  547.9 4.3 fusion.37
  552.2 116.0 %all-reduce.9.cloned.1.call-done = f32[4,128,128]{1,2,0:T(8,128)} async-done(((f32[4,128,128]{1,2,0:T(8,128)}), f32[4,128,128]{1,2,0:T(8,128)}) %all-reduce.9.cloned.1.call-update) | async-done | bytes 262160 | tf_op jit(solution)/shard_map/psum | solution.py:51
  668.3 8.5 copy.198
  676.7 1.8 gather_fusion.3
  678.6 0.7 convolution_subtract_fusion
  679.2 0.1 copy.203
  679.4 0.7 fusion.4
  680.1 47.9 %custom-call.22 = f32[4,128,128]{2,1,0:T(8,128)S(1)} custom-call(f32[4,128,128]{2,1,0:T(8,128)} %fusion.4), custom_call_target="Cholesky" | custom-call | tf_op jit(solution)/shard_map/vmap(jit(cholesky))/cholesky | solution.py:26
  728.3 39.3 %custom-call.23 = f32[4,1,128,128]{2,3,1,0:T(8,128)S(1)} custom-call(f32[4,1,128,128]{3,2,1,0:T(8,128)S(1)} %select_bitcast_fusion), custom_call_target="InvertDiagBlocksLowerTriangular" | custom-call | tf_op jit(solution)/shard_map/vmap(jit(_cho_solve))/triangular_solve | solution.py:27
  767.6 0.7 fusion.15
  768.3 0.6 fusion.2
  768.9 0.4 fusion
  769.3 2.0 fusion.38
  771.3 0.8 slice_bitcast_fusion
  772.1 4.6 collective-permute-start.1
  776.7 0.2 slice_select_fusion
  776.9 0.7 slice_bitcast_fusion.1
  777.6 1.9 collective-permute-start
  779.6 0.8 select_reduce_fusion.3
  780.4 75.6 %all-reduce = (f32[]{:T(128)}, f32[]{:T(128)}) all-reduce(f32[]{:T(128)} %get-tuple-element.15, f32[]{:T(128)} %get-tuple-element.14), channel_id=1, replica_groups=mesh['pair'=32,'row'=16] {'pair'}, use_global_device_ids=true, to_apply=%region_6.9 | all-reduce | flops 2 | bytes 16 | tf_op jit(solution)/shard_map/psum | solution.py:54
  857.2 1.2 slice.50
  858.5 1.4 maximum_select_fusion
  860.0 0.1 pad_maximum_fusion
  860.1 1.8 copy.206
  (48 shorter events, 1.6 us)
Async XLA Ops:
  37.3 57.0 %all-to-all-start = ((f32[32,128,128]{2,0,1:T(8,128)}), f32[32,128,128]{2,0,1:T(8,128)S(1)}, u32[]{:S(2)}, u32[]{:S(2)}) async-start(f32[32,128,128]{2,0,1:T(8,128)} %copy.174), calls=%async_computation | async-start | bytes 4194304 | tf_op jit(solution)/shard_map/all_to_all | solution.py:44
  47.1 174.2 %all-reduce.5.cloned.1.call-start = ((), (), s32[]{:S(2)}) async-start(), calls=%async_computation.1 | async-start | bytes 524288 | tf_op jit(solution)/shard_map/psum | solution.py:51
  94.3 1.3 copy-start.3
  101.7 343.1 %all-reduce.7.cloned.1.call-start = ((), (), s32[]{:S(2)}) async-start(), calls=%async_computation.2 | async-start | bytes 524288 | tf_op jit(solution)/shard_map/psum | solution.py:51
  221.3 10.3 %copy-start.4 = (f32[4,128,128]{1,2,0:T(8,128)S(1)}, f32[4,128,128]{1,2,0:T(8,128)}, u32[]{:S(2)}) copy-start(f32[4,128,128]{1,2,0:T(8,128)} %all-reduce.5.cloned.1.call-done) | copy-start | bytes 786436
  323.0 1.3 copy-start
  328.6 339.7 %all-reduce.9.cloned.1.call-start = ((), (), s32[]{:S(2)}) async-start(), calls=%async_computation.3 | async-start | bytes 524288 | tf_op jit(solution)/shard_map/psum | solution.py:51
  444.8 10.4 %copy-start.6 = (f32[4,128,128]{1,2,0:T(8,128)S(1)}, f32[4,128,128]{1,2,0:T(8,128)}, u32[]{:S(2)}) copy-start(f32[4,128,128]{1,2,0:T(8,128)} %all-reduce.7.cloned.1.call-done) | copy-start | bytes 786436
  668.3 10.3 %copy-start.5 = (f32[4,128,128]{1,2,0:T(8,128)S(1)}, f32[4,128,128]{1,2,0:T(8,128)}, u32[]{:S(2)}) copy-start(f32[4,128,128]{1,2,0:T(8,128)} %all-reduce.9.cloned.1.call-done) | copy-start | bytes 786436
  771.3 6.3 copy-start.1
  772.1 86.4 %collective-permute-start.1 = (f32[1024,64]{0,1:T(8,128)}, f32[1024,64]{0,1:T(8,128)}, u32[]{:S(2)}, u32[]{:S(2)}) collective-permute-start(f32[1024,64]{0,1:T(8,128)} %slice_bitcast_fusion), channel_id=1, source_target_pairs={{16,0},{32,16},{48,32},{64,48},{80,64},{96,80},{112,96},{128,112},... | collective-permute-start | bytes 786440 | tf_op jit(solution)/shard_map/ppermute | solution.py:13
  777.6 80.9 %collective-permute-start = (f32[1024,64]{0,1:T(8,128)}, f32[1024,64]{0,1:T(8,128)}, u32[]{:S(2)}, u32[]{:S(2)}) collective-permute-start(f32[1024,64]{0,1:T(8,128)} %slice_bitcast_fusion.1), channel_id=1, source_target_pairs={{0,16},{16,32},{32,48},{48,64},{64,80},{80,96},{96,112},{112,128},... | collective-permute-start | bytes 786440 | tf_op jit(solution)/shard_map/ppermute | solution.py:13
  779.5 79.0 %copy-start.2 = (f32[4,1024,128]{1,2,0:T(8,128)S(1)}, f32[4,1024,128]{1,2,0:T(8,128)}, u32[]{:S(2)}) copy-start(f32[4,1024,128]{1,2,0:T(8,128)} %copy-done.1) | copy-start | bytes 6291460
Sparse Core Ops, SparseCore 0:
  101.8 119.4 all-reduce.4
  328.7 116.0 all-reduce.6
  552.3 115.8 all-reduce.8
where the time goes:
time: 877 us; the launch traced here: 870 us
  waiting for transfers between devices  399 us (45%)
  other arithmetic  266 us (30%)
  blocking collectives  75.6 us (9%)
  local copies, waits for them, and re-layouts  68.9 us (8%)
  matrix products  27.1 us (3%)
  between operations  17 us (2%)
  starting transfers between devices  16.6 us (2%)
    psum x3, waiting for transfers between devices, on_device(): pair_gram = lax.psum(partial_value, 'row')  352 us
    another operation x10, other arithmetic, cayley(): factor = jnp.linalg.cholesky(system)  142 us
    another operation x7, other arithmetic, cayley(): return jax.scipy.linalg.cho_solve((factor, True), product.T).T  119 us
    psum x1, blocking collectives, on_device(): totals = lax.psum((off_part, diag_part), 'pair')  75.6 us
    all_to_all x1, waiting for transfers between devices, on_device(): lax.all_to_all(arranged, 'pair', split_axis=1, concat_axis=0, tiled=True)  46.9 us
    psum x3, local copies, waits for them, and re-layouts, on_device(): pair_gram = lax.psum(partial_value, 'row')  25.4 us
  transfers between devices with their start and end apart: 6, of which 4 were waited for; matrix products, arithmetic and copies ran while one was open for 0% of the time, Pallas kernels for 0%

commit v1 on v0

--- a/solution.py
+++ b/solution.py
@@ -41,7 +41,10 @@
     pair_width = 2 * BLOCK
     arranged = jnp.take(r_factor.reshape(rows_in, blocks, BLOCK), block_slots, axis=1)
     arranged = arranged.reshape(rows_in, blocks // 2, pair_width)
-    received = lax.all_to_all(arranged, "pair", split_axis=1, concat_axis=0, tiled=True)
+    received = jnp.concatenate(
+        lax.all_to_all(jnp.stack(jnp.split(arranged, lax.axis_size("pair"), axis=1)), "pair", 0, 0),
+        axis=0,
+    )
     column = jnp.transpose(received, (1, 0, 2))
     local_pairs = column.shape[0]
     rows_here = column.shape[1]

time: 877 us -> 894 us (1.019)
  local copies, waits for them, and re-layouts: 68.9 us -> 85.8 us
    unnamed x15 -> x44, local copies, waits for them, and re-layouts: 4.47 us -> 23.2 us
where the time goes in v1:
time: 894 us; the launch traced here: 887 us
  waiting for transfers between devices  399 us (45%)
  other arithmetic  266 us (30%)
  local copies, waits for them, and re-layouts  85.8 us (10%)
  blocking collectives  72.6 us (8%)
  matrix products  27.1 us (3%)
  starting transfers between devices  19.5 us (2%)
  between operations  17.1 us (2%)
    psum x3, waiting for transfers between devices, on_device(): pair_gram = lax.psum(partial_value, 'row')  352 us
    another operation x10, other arithmetic, cayley(): factor = jnp.linalg.cholesky(system)  142 us
    another operation x7, other arithmetic, cayley(): return jax.scipy.linalg.cho_solve((factor, True), product.T).T  119 us
    psum x1, blocking collectives, on_device(): totals = lax.psum((off_part, diag_part), 'pair')  72.6 us
    all_to_all x1, waiting for transfers between devices, on_device(): lax.all_to_all(jnp.stack(jnp.split(arranged, lax.axis_size('pair'), axis=...  46.9 us
    psum x3, local copies, waits for them, and re-layouts, on_device(): pair_gram = lax.psum(partial_value, 'row')  25.4 us
    unnamed x44, local copies, waits for them, and re-layouts  23.2 us
  transfers between devices with their start and end apart: 6, of which 4 were waited for; matrix products, arithmetic and copies ran while one was open for 0% of the time, Pallas kernels for 0%

profile of v1, /device:TPU:32, one launch (start us, length us, event | category | flops | bytes accessed | tf_op | source)
XLA Modules:
  0.0 886.8 jit_solution(4957659918106718826)
XLA Ops:
  7.2 0.7 compare_select_fusion
  7.8 0.7 compare_and_fusion
  8.5 4.3 reshape.90
  12.8 6.5 copy.155
  19.3 5.0 gather_fusion
  24.3 6.5 copy.156
  30.9 3.3 gather.17
  34.7 0.6 fusion.55
  35.4 0.6 fusion.54
  36.7 0.6 fusion.52
  38.0 0.6 fusion.50
  39.3 0.6 fusion.48
  40.6 0.6 fusion.46
  41.9 0.6 fusion.44
  43.2 0.6 fusion.42
  44.5 0.6 fusion.40
  45.8 0.6 fusion.38
  47.0 0.6 fusion.36
  48.3 0.6 fusion.34
  49.6 0.6 fusion.32
  50.9 0.6 fusion.30
  52.2 0.6 fusion.28
  53.5 0.6 fusion.26
  54.8 0.6 fusion.24
  55.5 9.9 %all-to-all-start = ((f32[32,32,4,128]{3,2,1,0:T(4,128)}), f32[32,32,4,128]{3,2,1,0:T(4,128)}, u32[]{:S(2)}, u32[]{:S(2)}) async-start(f32[32,32,4,128]{3,2,1,0:T(4,128)} %fusion.24), calls=%async_computation | async-start | bytes 4194304 | tf_op jit(solution)/shard_map/all_to_all | solution.py:45
  65.7 46.9 %all-to-all-done = f32[32,32,4,128]{3,2,1,0:T(4,128)} async-done(((f32[32,32,4,128]{3,2,1,0:T(4,128)}), f32[32,32,4,128]{3,2,1,0:T(4,128)}, u32[]{:S(2)}, u32[]{:S(2)}) %all-to-all-start) | async-done | bytes 2097184 | tf_op jit(solution)/shard_map/all_to_all | solution.py:45
  112.6 1.9 copy.157
  114.5 4.3 fusion.65
  118.8 119.6 %all-reduce.5.cloned.1.call-done = f32[4,128,128]{1,2,0:T(8,128)} async-done(((f32[4,128,128]{1,2,0:T(8,128)}), f32[4,128,128]{1,2,0:T(8,128)}) %all-reduce.5.cloned.1.call-update) | async-done | bytes 262160 | tf_op jit(solution)/shard_map/psum | solution.py:54
  238.5 8.5 copy.160
  246.9 1.8 gather_fusion.1
  248.8 0.7 convolution_subtract_fusion.2
  249.6 46.9 %custom-call.18 = f32[4,128,128]{2,1,0:T(8,128)S(1)} custom-call(f32[4,128,128]{2,1,0:T(8,128)S(1)} %fusion.14), custom_call_target="Cholesky" | custom-call | tf_op jit(solution)/shard_map/vmap(jit(cholesky))/cholesky | solution.py:26
  296.8 39.7 %custom-call.19 = f32[4,1,128,128]{2,3,1,0:T(8,128)S(1)} custom-call(f32[4,1,128,128]{3,2,1,0:T(8,128)S(1)} %select_bitcast_fusion.2), custom_call_target="InvertDiagBlocksLowerTriangular" | custom-call | tf_op jit(solution)/shard_map/vmap(jit(_cho_solve))/triangular_solve | solution.py:27
  336.5 0.6 fusion.19
  338.2 1.9 fusion.66
  340.2 1.3 copy-done
  341.5 4.3 fusion.67
  345.8 116.0 %all-reduce.7.cloned.1.call-done = f32[4,128,128]{1,2,0:T(8,128)} async-done(((f32[4,128,128]{1,2,0:T(8,128)}), f32[4,128,128]{1,2,0:T(8,128)}) %all-reduce.7.cloned.1.call-update) | async-done | bytes 262160 | tf_op jit(solution)/shard_map/psum | solution.py:54
  461.8 8.5 copy.170
  470.3 1.8 gather_fusion.2
  472.2 0.7 convolution_subtract_fusion.1
  473.0 46.9 %custom-call.20 = f32[4,128,128]{2,1,0:T(8,128)S(1)} custom-call(f32[4,128,128]{2,1,0:T(8,128)S(1)} %fusion.9), custom_call_target="Cholesky" | custom-call | tf_op jit(solution)/shard_map/vmap(jit(cholesky))/cholesky | solution.py:26
  520.2 39.5 %custom-call.21 = f32[4,1,128,128]{2,3,1,0:T(8,128)S(1)} custom-call(f32[4,1,128,128]{3,2,1,0:T(8,128)S(1)} %select_bitcast_fusion.1), custom_call_target="InvertDiagBlocksLowerTriangular" | custom-call | tf_op jit(solution)/shard_map/vmap(jit(_cho_solve))/triangular_solve | solution.py:27
  561.4 3.5 fusion.68
  564.9 4.3 fusion.69
  569.2 116.1 %all-reduce.9.cloned.1.call-done = f32[4,128,128]{1,2,0:T(8,128)} async-done(((f32[4,128,128]{1,2,0:T(8,128)}), f32[4,128,128]{1,2,0:T(8,128)}) %all-reduce.9.cloned.1.call-update) | async-done | bytes 262160 | tf_op jit(solution)/shard_map/psum | solution.py:54
  685.3 8.5 copy.180
  693.8 1.8 gather_fusion.3
  695.6 0.7 convolution_subtract_fusion
  696.4 0.7 fusion.4
  697.1 47.9 %custom-call.22 = f32[4,128,128]{2,1,0:T(8,128)S(1)} custom-call(f32[4,128,128]{2,1,0:T(8,128)} %fusion.4), custom_call_target="Cholesky" | custom-call | tf_op jit(solution)/shard_map/vmap(jit(cholesky))/cholesky | solution.py:26
  745.3 39.3 %custom-call.23 = f32[4,1,128,128]{2,3,1,0:T(8,128)S(1)} custom-call(f32[4,1,128,128]{3,2,1,0:T(8,128)S(1)} %select_bitcast_fusion), custom_call_target="InvertDiagBlocksLowerTriangular" | custom-call | tf_op jit(solution)/shard_map/vmap(jit(_cho_solve))/triangular_solve | solution.py:27
  784.7 0.7 fusion.15
  786.3 2.0 fusion.70
  788.3 0.8 slice_bitcast_fusion
  789.4 0.7 slice_bitcast_fusion.1
  790.1 3.4 collective-permute-start
  793.5 5.9 collective-permute-start.1
  799.4 0.8 select_reduce_fusion.3
  800.2 72.6 %all-reduce = (f32[]{:T(128)}, f32[]{:T(128)}) all-reduce(f32[]{:T(128)} %get-tuple-element.13, f32[]{:T(128)} %get-tuple-element.12), channel_id=1, replica_groups=mesh['pair'=32,'row'=16] {'pair'}, use_global_device_ids=true, to_apply=%region_6.9 | all-reduce | flops 2 | bytes 16 | tf_op jit(solution)/shard_map/psum | solution.py:57
  874.1 1.2 slice.50
  875.3 1.4 maximum_select_fusion
  876.9 1.8 copy.188
  (77 shorter events, 16.3 us)
Async XLA Ops:
  55.5 57.1 %all-to-all-start = ((f32[32,32,4,128]{3,2,1,0:T(4,128)}), f32[32,32,4,128]{3,2,1,0:T(4,128)}, u32[]{:S(2)}, u32[]{:S(2)}) async-start(f32[32,32,4,128]{3,2,1,0:T(4,128)} %fusion.24), calls=%async_computation | async-start | bytes 4194304 | tf_op jit(solution)/shard_map/all_to_all | solution.py:45
  65.4 173.1 %all-reduce.5.cloned.1.call-start = ((), (), s32[]{:S(2)}) async-start(), calls=%async_computation.1 | async-start | bytes 524288 | tf_op jit(solution)/shard_map/psum | solution.py:54
  118.8 343.0 %all-reduce.7.cloned.1.call-start = ((), (), s32[]{:S(2)}) async-start(), calls=%async_computation.2 | async-start | bytes 524288 | tf_op jit(solution)/shard_map/psum | solution.py:54
  238.5 10.3 %copy-start.3 = (f32[4,128,128]{1,2,0:T(8,128)S(1)}, f32[4,128,128]{1,2,0:T(8,128)}, u32[]{:S(2)}) copy-start(f32[4,128,128]{1,2,0:T(8,128)} %all-reduce.5.cloned.1.call-done) | copy-start | bytes 786436
  340.1 1.3 copy-start
  345.8 339.5 %all-reduce.9.cloned.1.call-start = ((), (), s32[]{:S(2)}) async-start(), calls=%async_computation.3 | async-start | bytes 524288 | tf_op jit(solution)/shard_map/psum | solution.py:54
  461.8 10.4 %copy-start.5 = (f32[4,128,128]{1,2,0:T(8,128)S(1)}, f32[4,128,128]{1,2,0:T(8,128)}, u32[]{:S(2)}) copy-start(f32[4,128,128]{1,2,0:T(8,128)} %all-reduce.7.cloned.1.call-done) | copy-start | bytes 786436
  685.3 10.3 %copy-start.4 = (f32[4,128,128]{1,2,0:T(8,128)S(1)}, f32[4,128,128]{1,2,0:T(8,128)}, u32[]{:S(2)}) copy-start(f32[4,128,128]{1,2,0:T(8,128)} %all-reduce.9.cloned.1.call-done) | copy-start | bytes 786436
  788.3 1.8 copy-start.1
  790.1 85.2 %collective-permute-start = (f32[1024,64]{0,1:T(8,128)}, f32[1024,64]{0,1:T(8,128)}, u32[]{:S(2)}, u32[]{:S(2)}) collective-permute-start(f32[1024,64]{0,1:T(8,128)} %slice_bitcast_fusion.1), channel_id=1, source_target_pairs={{0,16},{16,32},{32,48},{48,64},{64,80},{80,96},{96,112},{112,128},... | collective-permute-start | bytes 786440 | tf_op jit(solution)/shard_map/ppermute | solution.py:13
  793.5 81.9 %copy-start.2 = (f32[4,1024,128]{1,2,0:T(8,128)S(1)}, f32[4,1024,128]{1,2,0:T(8,128)}, u32[]{:S(2)}) copy-start(f32[4,1024,128]{1,2,0:T(8,128)} %copy-done.1) | copy-start | bytes 6291460
  793.5 81.9 %collective-permute-start.1 = (f32[1024,64]{0,1:T(8,128)}, f32[1024,64]{0,1:T(8,128)}, u32[]{:S(2)}, u32[]{:S(2)}) collective-permute-start(f32[1024,64]{0,1:T(8,128)} %slice_bitcast_fusion), channel_id=1, source_target_pairs={{16,0},{32,16},{48,32},{64,48},{80,64},{96,80},{112,96},{128,112},... | collective-permute-start | bytes 786440 | tf_op jit(solution)/shard_map/ppermute | solution.py:13
Sparse Core Ops, SparseCore 0:
  118.9 119.5 all-reduce.4
  345.9 115.8 all-reduce.6
  569.3 115.9 all-reduce.8
